TPU v7x, 32 devices: a whole 2x2x4 slice. The times are simulated.
32 devices in a mesh: sub: 8 (over z, y), grp: 4 (over x, core).
Axes of the slice: x: 2, y: 2, z: 4, core: 2. Of those that a mesh axis runs over, the one named last changes fastest.
Arguments:
- schur: bfloat16 [8, 2048, 2048], P('sub', 'grp'), may hold values from -0.125 to 0.125
- rhs: float32 [8, 2048, 192], P('sub', 'grp'), may hold values from -6 to 6
- start: float32 [8, 2048, 192], P('sub', 'grp'), may hold values from -6 to 6
- project: bfloat16 [8, 32, 4096], P('sub', 'grp'), may hold values from -0.75 to 0.75
- coarse_basis: bfloat16 [8, 8, 2048], P('sub', None, 'grp'), may hold values from -0.375 to 0.375
- owner_of_face: int32 [8, 32, 1], replicated, may hold values from 0 to 4; in each aligned block of 32 rows (0 to 31, 32 to 63, ..., all dimensions but the last counted through in order) at most 8 rows name the same one
- mortar_of_face: int32 [8, 32], replicated, may hold values from 0 to 15
- mortar_order: int32 [8, 16], replicated, may hold values from 3 to 7
- subdomain_map: int32 [8], replicated, may hold values from 0 to 7, each once
- vertex_ids: int32 [8, 8], replicated, may hold values from 0 to 15, all different within a row
Outputs:
- solution: float32 [8, 2048, 192], P('sub', 'grp')
Inputs may be any that keep to these rules, and one draw needn't show every extreme that they name: `owner_of_face`: the 32 faces of one subdomain name one offset at most 8 times. `mortar_of_face`: faces with the same owner and the same number lie on one mortar. `mortar_order`: row o holds the orders of the mortars owned by index o. `subdomain_map`: each subdomain once. `vertex_ids`: the 8 vertices of a subdomain differ; every vertex belongs to some subdomain.
All inputs are finite; a program needn't handle non-finite values.
Results may differ from a plain program's by a relative error of at most 0.0031.
Values may be sent and summed in bfloat16 or wider, within the bound.
No kernel may reach another device: no remote copies, remote signals or barrier semaphores. Data moves between devices by JAX's collectives and lax.ppermute only.
A program may use at most 64 MiB of HBM per device.

v0:
```python
import jax
import jax.numpy as jnp
from jax import lax
from jax.sharding import PartitionSpec as P

DEG = 8
FPTS = 64
MODES = 64
MORT_OWN = 16
ITERS = 2
REACH = 2
CAP = 8
relax_weight = 0.5
coarse_weight = 0.5


def passed_along(value, axis, steps):
    count = lax.axis_size(axis)
    pairs = [(source, (source + steps) % count) for source in range(count)]
    return lax.ppermute(value, axis, pairs)


def body(
    schur,
    rhs,
    start,
    project,
    coarse_basis,
    owner_of_face,
    mortar_of_face,
    mortar_order,
    subdomain_map,
    vertex_ids,
):
    highest = lax.Precision.HIGHEST
    contract_first = (((0,), (0,)), ((), ()))
    sub_count = lax.axis_size("sub")
    position = lax.axis_index("sub")
    all_faces = owner_of_face.shape[1]
    own_faces = project.shape[1]
    own_rows = schur.shape[1]
    neighbours = 2 * REACH + 1
    capacity = CAP
    vertices = 2 * sub_count
    held = jnp.take(owner_of_face[:, :, 0], subdomain_map, axis=0)
    mortar_local = jnp.take(mortar_of_face, subdomain_map, axis=0)
    face_index = jnp.arange(all_faces, dtype=jnp.int32)
    earlier = face_index[None, :] < face_index[:, None]
    ranks = jnp.sum(
        ((held[:, :, None] == held[:, None, :]) & earlier[None, :, :]).astype(jnp.int32), axis=2
    )
    my_held = lax.dynamic_index_in_dim(held, position, 0, keepdims=False)
    my_ranks = lax.dynamic_index_in_dim(ranks, position, 0, keepdims=False)
    slot_ids = my_held * capacity + my_ranks
    send_table = (
        jnp.arange(neighbours * capacity, dtype=jnp.int32)[:, None] == slot_ids[None, :]
    ).astype(jnp.bfloat16)
    links = jnp.arange(neighbours, dtype=jnp.int32)
    senders = jnp.mod(position - links + REACH, sub_count)
    from_held = jnp.take(held, senders, axis=0)
    from_mortar = jnp.take(mortar_local, senders, axis=0)
    from_ranks = jnp.take(ranks, senders, axis=0)
    incoming = (from_held == links[:, None]).astype(jnp.float32)
    mortar_hot = (
        from_mortar[:, :, None] == jnp.arange(MORT_OWN, dtype=jnp.int32)[None, None, :]
    ).astype(jnp.float32)
    rank_hot = (
        from_ranks[:, :, None] == jnp.arange(capacity, dtype=jnp.int32)[None, None, :]
    ).astype(jnp.float32)
    counts = jnp.einsum("jfk,jf->k", mortar_hot, incoming)
    degree = jnp.arange(MODES, dtype=jnp.int32)
    orders = lax.dynamic_index_in_dim(mortar_order, position, 0, keepdims=False)[:, None]
    keep_mask = ((degree[None, :] // DEG <= orders) & (degree[None, :] % DEG <= orders)).astype(
        jnp.float32
    )
    divisor = jnp.maximum(counts, 1.0)
    joined = jnp.einsum("jfk,jfc->kjc", mortar_hot * incoming[:, :, None], rank_hot)
    owner_table = joined.reshape(MORT_OWN, neighbours * capacity).astype(jnp.bfloat16)
    my_corners = lax.dynamic_index_in_dim(
        jnp.take(vertex_ids, subdomain_map, axis=0), position, 0, keepdims=False
    )
    corner_hot = (my_corners[:, None] == jnp.arange(vertices, dtype=jnp.int32)[None, :]).astype(
        jnp.float32
    )
    coarse_wide = coarse_basis[0].astype(jnp.float32)
    tables = project[0].reshape(own_faces, MODES, FPTS)
    matrix = schur[0]
    target = rhs[0]
    traces = start[0]
    for repeat in range(ITERS):
        trace_b = traces.astype(jnp.bfloat16)
        product = jnp.dot(
            matrix,
            lax.all_gather(trace_b, "grp", axis=0, tiled=True),
            preferred_element_type=jnp.float32,
        )
        residual = (product - target).astype(jnp.bfloat16)
        face_res = residual.reshape(own_faces, FPTS, -1)
        coeffs = jnp.einsum(
            "fmp,fpr->fmr", tables, face_res, preferred_element_type=jnp.float32
        ).astype(jnp.bfloat16)
        grouped = lax.all_to_all(coeffs, "grp", split_axis=2, concat_axis=0, tiled=True)
        part_rhs = grouped.shape[2]
        payload = grouped.reshape(all_faces, MODES * part_rhs)
        outgoing = jnp.dot(send_table, payload, preferred_element_type=jnp.float32).astype(
            jnp.bfloat16
        )
        blocks = outgoing.reshape(neighbours, capacity, -1)
        arrivals = []
        for link in range(neighbours):
            arrivals.append(passed_along(blocks[link], "sub", link - REACH))
        arrived = jnp.concatenate(arrivals, axis=0)
        mortar_sums = jnp.dot(owner_table, arrived, preferred_element_type=jnp.float32)
        shaped = mortar_sums.reshape(MORT_OWN, MODES, part_rhs) / divisor[:, None, None]
        shaped = shaped * keep_mask[:, :, None]
        averages = shaped.reshape(MORT_OWN, MODES * part_rhs).astype(jnp.bfloat16)
        replies = lax.dot_general(
            owner_table, averages, contract_first, preferred_element_type=jnp.float32
        ).astype(jnp.bfloat16)
        reply_blocks = replies.reshape(neighbours, capacity, -1)
        answers = []
        for link in range(neighbours):
            answers.append(passed_along(reply_blocks[link], "sub", REACH - link))
        answered = jnp.concatenate(answers, axis=0)
        own_back = lax.dot_general(
            send_table, answered, contract_first, preferred_element_type=jnp.float32
        ).astype(jnp.bfloat16)
        returned = lax.all_to_all(
            own_back.reshape(all_faces, MODES, part_rhs),
            "grp",
            split_axis=0,
            concat_axis=2,
            tiled=True,
        )
        lifted = jnp.einsum(
            "fmp,fmr->fpr", tables, returned, preferred_element_type=jnp.float32
        ).reshape(own_rows, -1)
        partial_value = jnp.dot(coarse_wide, lifted, precision=highest)
        spread = lax.dot_general(corner_hot, partial_value, contract_first, precision=highest)
        vertex = lax.psum(spread, ("sub", "grp"))
        picked = jnp.dot(corner_hot, vertex, precision=highest)
        coarse_corr = lax.dot_general(coarse_wide, picked, contract_first, precision=highest)
        traces = traces - relax_weight * lifted - coarse_weight * coarse_corr
    return traces[None]


def solution(mesh):
    return jax.shard_map(
        body,
        mesh=mesh,
        in_specs=(
            P("sub", "grp", None),
            P("sub", "grp", None),
            P("sub", "grp", None),
            P("sub", "grp", None),
            P("sub", None, "grp"),
            P(),
            P(),
            P(),
            P(),
            P(),
        ),
        out_specs=P("sub", "grp", None),
        check_vma=False,
    )
```

profile of v0, /device:TPU:10, one launch (start us, length us, event | category | flops | bytes accessed | tf_op | source)
XLA Modules:
  0.0 199.1 jit_solution(15513312980948887110)
XLA Ops:
  0.0 1.2 reshape_squeeze.3
  1.2 1.0 bitcast_convert_fusion
  2.2 8.2 %all_gather.6 = bf16[2048,192]{0,1:T(8,128)(2,1)S(1)} all-gather(bf16[512,192]{0,1:T(8,128)(2,1)S(1)} %bitcast_convert_fusion), channel_id=1, replica_groups=mesh['sub'=8,'grp'=4] {'grp'}, dimensions={0}, use_global_device_ids=true | all-gather | bytes 983040 | tf_op jit(solution)/shard_map/all_gather | solution.py:94
  10.4 1.8 fusion.20
  12.9 1.0 reshape.310
  13.9 4.3 %all-to-all-start = ((bf16[4,2,12288]{2,1,0:T(2,128)(2,1)}), bf16[4,2,12288]{2,1,0:T(2,128)(2,1)S(1)}, u32[]{:S(2)}, u32[]{:S(2)}) async-start(bf16[4,2,12288]{2,1,0:T(2,128)(2,1)} %reshape.310), calls=%async_computation | async-start | bytes 393216 | tf_op jit(solution)/shard_map/all_to_all | solution.py:102
  24.8 1.6 collective-permute-start.4
  26.4 1.5 collective-permute-start.3
  27.9 1.6 collective-permute-start.1
  29.5 2.9 %collective-permute-done.1 = bf16[8,3072]{1,0:T(8,128)(2,1)S(1)} collective-permute-done((bf16[8,3072]{1,0:T(8,128)(2,1)S(1)}, bf16[8,3072]{1,0:T(8,128)(2,1)S(1)}, u32[]{:S(2)}, u32[]{:S(2)}) %collective-permute-start.1) | collective-permute-done | bytes 49184 | tf_op jit(solution)/shard_map/ppermute | solution.py:20
  35.3 1.9 collective-permute-start.5
  37.7 0.9 collective-permute-start.9
  38.7 4.3 %collective-permute-start.8 = (bf16[8,3072]{1,0:T(8,128)(2,1)S(1)}, bf16[8,3072]{1,0:T(8,128)(2,1)S(1)}, u32[]{:S(2)}, u32[]{:S(2)}) collective-permute-start(bf16[8,3072]{1,0:T(8,128)(2,1)S(1)} %get-tuple-element.20), channel_id=1, source_target_pairs={{0,28},{4,0},{8,4},{12,8},{16,12},{20,16},{24,20},{28,24},{1,29},{... | collective-permute-start | bytes 147464 | tf_op jit(solution)/shard_map/ppermute | solution.py:20
  43.0 5.0 %collective-permute-done.6 = bf16[8,3072]{1,0:T(8,128)(2,1)S(1)} collective-permute-done((bf16[8,3072]{1,0:T(8,128)(2,1)S(1)}, bf16[8,3072]{1,0:T(8,128)(2,1)S(1)}, u32[]{:S(2)}, u32[]{:S(2)}) %collective-permute-start.6) | collective-permute-done | bytes 49184 | tf_op jit(solution)/shard_map/ppermute | solution.py:20
  49.1 1.0 reshape.312
  50.1 4.3 %all-to-all-start.1 = ((bf16[4,2,12288]{2,1,0:T(2,128)(2,1)}), bf16[4,2,12288]{2,1,0:T(2,128)(2,1)S(1)}, u32[]{:S(2)}, u32[]{:S(2)}) async-start(bf16[4,2,12288]{2,1,0:T(2,128)(2,1)} %reshape.312), calls=%async_computation.1 | async-start | bytes 393216 | tf_op jit(solution)/shard_map/all_to_all | solution.py:128
  55.1 2.9 %all-to-all-done.1 = bf16[4,2,12288]{2,1,0:T(2,128)(2,1)S(1)} async-done(((bf16[4,2,12288]{2,1,0:T(2,128)(2,1)}), bf16[4,2,12288]{2,1,0:T(2,128)(2,1)S(1)}, u32[]{:S(2)}, u32[]{:S(2)}) %all-to-all-start.1) | async-done | bytes 196640 | tf_op jit(solution)/shard_map/all_to_all | solution.py:128
  59.5 43.4 %psum.14 = f32[16,192]{1,0:T(8,128)S(1)} all-reduce(f32[16,192]{1,0:T(8,128)S(1)} %fusion.55), channel_id=1, replica_groups=mesh['sub'=8,'grp'=4] {'sub','grp'}, use_global_device_ids=true, to_apply=%region_1.0 | all-reduce | flops 3072 | bytes 24576 | tf_op jit(solution)/shard_map/psum | solution.py:140
  103.1 1.1 fusion.72
  104.2 7.2 %all_gather.7 = bf16[2048,192]{0,1:T(8,128)(2,1)S(1)} all-gather(bf16[512,192]{0,1:T(8,128)(2,1)S(1)} %get-tuple-element.33), channel_id=1, replica_groups=mesh['sub'=8,'grp'=4] {'grp'}, dimensions={0}, use_global_device_ids=true | all-gather | bytes 983040 | tf_op jit(solution)/shard_map/all_gather | solution.py:94
  111.4 0.8 fusion.23
  113.2 8.0 %all_to_all.66 = bf16[4,2,12288]{2,1,0:T(2,128)(2,1)S(1)} all-to-all(bf16[4,2,12288]{2,1,0:T(2,128)(2,1)S(1)} %reshape.314), channel_id=1, replica_groups=mesh['sub'=8,'grp'=4] {'grp'}, dimensions={0} | all-to-all | bytes 393216 | tf_op jit(solution)/shard_map/all_to_all | solution.py:102
  122.9 2.0 %collective-permute-start.14 = (bf16[8,3072]{1,0:T(8,128)(2,1)S(1)}, bf16[8,3072]{1,0:T(8,128)(2,1)S(1)}, u32[]{:S(2)}, u32[]{:S(2)}) collective-permute-start(bf16[8,3072]{1,0:T(8,128)(2,1)S(1)} %get-tuple-element.14), channel_id=1, source_target_pairs={{0,8},{4,12},{8,16},{12,20},{16,24},{20,28},{24,0},{28,4},{1,9},{5... | collective-permute-start | bytes 147464 | tf_op jit(solution)/shard_map/ppermute | solution.py:20
  125.7 2.2 %collective-permute-start.11 = (bf16[8,3072]{1,0:T(8,128)(2,1)S(1)}, bf16[8,3072]{1,0:T(8,128)(2,1)S(1)}, u32[]{:S(2)}, u32[]{:S(2)}) collective-permute-start(bf16[8,3072]{1,0:T(8,128)(2,1)S(1)} %get-tuple-element.17), channel_id=1, source_target_pairs={{0,28},{4,0},{8,4},{12,8},{16,12},{20,16},{24,20},{28,24},{1,29},{... | collective-permute-start | bytes 147464 | tf_op jit(solution)/shard_map/ppermute | solution.py:20
  127.9 2.4 %collective-permute-done.11 = bf16[8,3072]{1,0:T(8,128)(2,1)S(1)} collective-permute-done((bf16[8,3072]{1,0:T(8,128)(2,1)S(1)}, bf16[8,3072]{1,0:T(8,128)(2,1)S(1)}, u32[]{:S(2)}, u32[]{:S(2)}) %collective-permute-start.11) | collective-permute-done | bytes 49184 | tf_op jit(solution)/shard_map/ppermute | solution.py:20
  132.5 0.9 collective-permute-start.15
  133.4 1.2 collective-permute-start.19
  134.6 4.4 %collective-permute-start.18 = (bf16[8,3072]{1,0:T(8,128)(2,1)S(1)}, bf16[8,3072]{1,0:T(8,128)(2,1)S(1)}, u32[]{:S(2)}, u32[]{:S(2)}) collective-permute-start(bf16[8,3072]{1,0:T(8,128)(2,1)S(1)} %get-tuple-element.10), channel_id=1, source_target_pairs={{0,28},{4,0},{8,4},{12,8},{16,12},{20,16},{24,20},{28,24},{1,29},{... | collective-permute-start | bytes 147464 | tf_op jit(solution)/shard_map/ppermute | solution.py:20
  139.0 5.0 %collective-permute-done.16 = bf16[8,3072]{1,0:T(8,128)(2,1)S(1)} collective-permute-done((bf16[8,3072]{1,0:T(8,128)(2,1)S(1)}, bf16[8,3072]{1,0:T(8,128)(2,1)S(1)}, u32[]{:S(2)}, u32[]{:S(2)}) %collective-permute-start.16) | collective-permute-done | bytes 49184 | tf_op jit(solution)/shard_map/ppermute | solution.py:20
  145.4 7.6 %all_to_all.67 = bf16[4,2,12288]{2,1,0:T(2,128)(2,1)S(1)} all-to-all(bf16[4,2,12288]{2,1,0:T(2,128)(2,1)S(1)} %reshape.316), channel_id=1, replica_groups=mesh['sub'=8,'grp'=4] {'grp'}, dimensions={0} | all-to-all | bytes 393216 | tf_op jit(solution)/shard_map/all_to_all | solution.py:128
  154.5 43.3 %psum.15 = f32[16,192]{1,0:T(8,128)S(1)} all-reduce(f32[16,192]{1,0:T(8,128)S(1)} %fusion.53), channel_id=1, replica_groups=mesh['sub'=8,'grp'=4] {'sub','grp'}, use_global_device_ids=true, to_apply=%region_2.5 | all-reduce | flops 3072 | bytes 24576 | tf_op jit(solution)/shard_map/psum | solution.py:140
  197.9 1.1 fusion.6
  (154 shorter events, 22.4 us)
Async XLA Ops:
  0.0 10.4 %copy-start = (bf16[1,512,2048]{2,1,0:T(8,128)(2,1)S(1)}, bf16[1,512,2048]{2,1,0:T(8,128)(2,1)}, u32[]{:S(2)}) copy-start(bf16[1,512,2048]{2,1,0:T(8,128)(2,1)} %param.14) | copy-start | bytes 6291460
  13.9 8.7 %all-to-all-start = ((bf16[4,2,12288]{2,1,0:T(2,128)(2,1)}), bf16[4,2,12288]{2,1,0:T(2,128)(2,1)S(1)}, u32[]{:S(2)}, u32[]{:S(2)}) async-start(bf16[4,2,12288]{2,1,0:T(2,128)(2,1)} %reshape.310), calls=%async_computation | async-start | bytes 393216 | tf_op jit(solution)/shard_map/all_to_all | solution.py:102
  22.4 12.6 %copy-start.8 = (bf16[5,8,16]{2,1,0:T(8,128)(2,1)}, bf16[5,8,16]{2,1,0:T(8,128)(2,1)S(1)}, u32[]{:S(2)}) copy-start(bf16[5,8,16]{2,1,0:T(8,128)(2,1)S(1)} %convolution_convert_fusion.8) | copy-start | bytes 3844
  22.5 11.6 %copy-start.10 = (f32[16,64]{1,0:T(8,128)}, f32[16,64]{1,0:T(8,128)S(1)}, u32[]{:S(2)}) copy-start(f32[16,64]{1,0:T(8,128)S(1)} %and_convert_fusion) | copy-start | bytes 12292
  24.2 5.3 %collective-permute-start = (bf16[8,3072]{1,0:T(8,128)(2,1)S(1)}, bf16[8,3072]{1,0:T(8,128)(2,1)S(1)}, u32[]{:S(2)}, u32[]{:S(2)}) collective-permute-start(bf16[8,3072]{1,0:T(8,128)(2,1)S(1)} %get-tuple-element.28), channel_id=1, source_target_pairs={{0,24},{4,28},{8,0},{12,4},{16,8},{20,12},{24,16},{28,20},{1,25},{... | collective-permute-start | bytes 147464 | tf_op jit(solution)/shard_map/ppermute | solution.py:20
  24.8 9.9 %copy-start.14 = (f32[16]{0:T(128)}, f32[16]{0:T(128)S(1)}, u32[]{:S(2)}) copy-start(f32[16]{0:T(128)S(1)} %fusion.30) | copy-start | bytes 196
  24.8 8.3 %collective-permute-start.4 = (bf16[8,3072]{1,0:T(8,128)(2,1)S(1)}, bf16[8,3072]{1,0:T(8,128)(2,1)S(1)}, u32[]{:S(2)}, u32[]{:S(2)}) collective-permute-start(bf16[8,3072]{1,0:T(8,128)(2,1)S(1)} %get-tuple-element.24), channel_id=1, source_target_pairs={{0,8},{4,12},{8,16},{12,20},{16,24},{20,28},{24,0},{28,4},{1,9},{5... | collective-permute-start | bytes 147464 | tf_op jit(solution)/shard_map/ppermute | solution.py:20
  26.4 6.7 %collective-permute-start.3 = (bf16[8,3072]{1,0:T(8,128)(2,1)S(1)}, bf16[8,3072]{1,0:T(8,128)(2,1)S(1)}, u32[]{:S(2)}, u32[]{:S(2)}) collective-permute-start(bf16[8,3072]{1,0:T(8,128)(2,1)S(1)} %get-tuple-element.25), channel_id=1, source_target_pairs={{0,4},{4,8},{8,12},{12,16},{16,20},{20,24},{24,28},{28,0},{1,5},{5... | collective-permute-start | bytes 147464 | tf_op jit(solution)/shard_map/ppermute | solution.py:20
  27.9 4.5 %collective-permute-start.2 = (bf16[8,3072]{1,0:T(8,128)(2,1)S(1)}, bf16[8,3072]{1,0:T(8,128)(2,1)S(1)}, u32[]{:S(2)}, u32[]{:S(2)}) collective-permute-start(bf16[8,3072]{1,0:T(8,128)(2,1)S(1)} %get-tuple-element.26), channel_id=1, source_target_pairs={{0,0},{4,4},{8,8},{12,12},{16,16},{20,20},{24,24},{28,28},{1,1},{5... | collective-permute-start | bytes 147464 | tf_op jit(solution)/shard_map/ppermute | solution.py:20
  27.9 4.5 %collective-permute-start.1 = (bf16[8,3072]{1,0:T(8,128)(2,1)S(1)}, bf16[8,3072]{1,0:T(8,128)(2,1)S(1)}, u32[]{:S(2)}, u32[]{:S(2)}) collective-permute-start(bf16[8,3072]{1,0:T(8,128)(2,1)S(1)} %get-tuple-element.27), channel_id=1, source_target_pairs={{0,28},{4,0},{8,4},{12,8},{16,12},{20,16},{24,20},{28,24},{1,29},{... | collective-permute-start | bytes 147464 | tf_op jit(solution)/shard_map/ppermute | solution.py:20
  35.3 7.7 %collective-permute-start.5 = (bf16[8,3072]{1,0:T(8,128)(2,1)S(1)}, bf16[8,3072]{1,0:T(8,128)(2,1)S(1)}, u32[]{:S(2)}, u32[]{:S(2)}) collective-permute-start(bf16[8,3072]{1,0:T(8,128)(2,1)S(1)} %get-tuple-element.23), channel_id=1, source_target_pairs={{0,8},{4,12},{8,16},{12,20},{16,24},{20,28},{24,0},{28,4},{1,9},{5... | collective-permute-start | bytes 147464 | tf_op jit(solution)/shard_map/ppermute | solution.py:20
  37.7 10.3 %collective-permute-start.9 = (bf16[8,3072]{1,0:T(8,128)(2,1)S(1)}, bf16[8,3072]{1,0:T(8,128)(2,1)S(1)}, u32[]{:S(2)}, u32[]{:S(2)}) collective-permute-start(bf16[8,3072]{1,0:T(8,128)(2,1)S(1)} %get-tuple-element.19), channel_id=1, source_target_pairs={{0,24},{4,28},{8,0},{12,4},{16,8},{20,12},{24,16},{28,20},{1,25},{... | collective-permute-start | bytes 147464 | tf_op jit(solution)/shard_map/ppermute | solution.py:20
  38.7 9.3 %collective-permute-start.8 = (bf16[8,3072]{1,0:T(8,128)(2,1)S(1)}, bf16[8,3072]{1,0:T(8,128)(2,1)S(1)}, u32[]{:S(2)}, u32[]{:S(2)}) collective-permute-start(bf16[8,3072]{1,0:T(8,128)(2,1)S(1)} %get-tuple-element.20), channel_id=1, source_target_pairs={{0,28},{4,0},{8,4},{12,8},{16,12},{20,16},{24,20},{28,24},{1,29},{... | collective-permute-start | bytes 147464 | tf_op jit(solution)/shard_map/ppermute | solution.py:20
  43.0 5.0 %collective-permute-start.7 = (bf16[8,3072]{1,0:T(8,128)(2,1)S(1)}, bf16[8,3072]{1,0:T(8,128)(2,1)S(1)}, u32[]{:S(2)}, u32[]{:S(2)}) collective-permute-start(bf16[8,3072]{1,0:T(8,128)(2,1)S(1)} %get-tuple-element.21), channel_id=1, source_target_pairs={{0,0},{4,4},{8,8},{12,12},{16,16},{20,20},{24,24},{28,28},{1,1},{5... | collective-permute-start | bytes 147464 | tf_op jit(solution)/shard_map/ppermute | solution.py:20
  43.0 5.0 %collective-permute-start.6 = (bf16[8,3072]{1,0:T(8,128)(2,1)S(1)}, bf16[8,3072]{1,0:T(8,128)(2,1)S(1)}, u32[]{:S(2)}, u32[]{:S(2)}) collective-permute-start(bf16[8,3072]{1,0:T(8,128)(2,1)S(1)} %get-tuple-element.22), channel_id=1, source_target_pairs={{0,4},{4,8},{8,12},{12,16},{16,20},{20,24},{24,28},{28,0},{1,5},{5... | collective-permute-start | bytes 147464 | tf_op jit(solution)/shard_map/ppermute | solution.py:20
  49.1 9.8 %copy-start.7 = (bf16[1,8,512]{2,1,0:T(8,128)(2,1)S(1)}, bf16[1,8,512]{2,1,0:T(8,128)(2,1)}, u32[]{:S(2)}) copy-start(bf16[1,8,512]{2,1,0:T(8,128)(2,1)} %param.18) | copy-start | bytes 24580
  50.1 7.9 %all-to-all-start.1 = ((bf16[4,2,12288]{2,1,0:T(2,128)(2,1)}), bf16[4,2,12288]{2,1,0:T(2,128)(2,1)S(1)}, u32[]{:S(2)}, u32[]{:S(2)}) async-start(bf16[4,2,12288]{2,1,0:T(2,128)(2,1)} %reshape.312), calls=%async_computation.1 | async-start | bytes 393216 | tf_op jit(solution)/shard_map/all_to_all | solution.py:128
  54.4 48.7 %copy-start.1 = (f32[1,512,192]{1,2,0:T(8,128)S(1)}, f32[1,512,192]{1,2,0:T(8,128)}, u32[]{:S(2)}) copy-start(f32[1,512,192]{1,2,0:T(8,128)} %param.16) | copy-start | bytes 1179652
  121.8 9.6 %copy-start.9 = (bf16[5,8,16]{2,1,0:T(8,128)(2,1)S(1)}, bf16[5,8,16]{2,1,0:T(8,128)(2,1)}, u32[]{:S(2)}) copy-start(bf16[5,8,16]{2,1,0:T(8,128)(2,1)} %copy-done.8) | copy-start | bytes 3844
  121.8 9.6 %copy-start.11 = (f32[16,64]{1,0:T(8,128)S(1)}, f32[16,64]{1,0:T(8,128)}, u32[]{:S(2)}) copy-start(f32[16,64]{1,0:T(8,128)} %copy-done.10) | copy-start | bytes 12292
  121.8 9.6 %copy-start.15 = (f32[16]{0:T(128)S(1)}, f32[16]{0:T(128)}, u32[]{:S(2)}) copy-start(f32[16]{0:T(128)} %copy-done.14) | copy-start | bytes 196
  122.9 5.0 %collective-permute-start.10 = (bf16[8,3072]{1,0:T(8,128)(2,1)S(1)}, bf16[8,3072]{1,0:T(8,128)(2,1)S(1)}, u32[]{:S(2)}, u32[]{:S(2)}) collective-permute-start(bf16[8,3072]{1,0:T(8,128)(2,1)S(1)} %get-tuple-element.18), channel_id=1, source_target_pairs={{0,24},{4,28},{8,0},{12,4},{16,8},{20,12},{24,16},{28,20},{1,25},{... | collective-permute-start | bytes 147464 | tf_op jit(solution)/shard_map/ppermute | solution.py:20
  122.9 7.4 %collective-permute-start.14 = (bf16[8,3072]{1,0:T(8,128)(2,1)S(1)}, bf16[8,3072]{1,0:T(8,128)(2,1)S(1)}, u32[]{:S(2)}, u32[]{:S(2)}) collective-permute-start(bf16[8,3072]{1,0:T(8,128)(2,1)S(1)} %get-tuple-element.14), channel_id=1, source_target_pairs={{0,8},{4,12},{8,16},{12,20},{16,24},{20,28},{24,0},{28,4},{1,9},{5... | collective-permute-start | bytes 147464 | tf_op jit(solution)/shard_map/ppermute | solution.py:20
  124.9 5.4 %collective-permute-start.13 = (bf16[8,3072]{1,0:T(8,128)(2,1)S(1)}, bf16[8,3072]{1,0:T(8,128)(2,1)S(1)}, u32[]{:S(2)}, u32[]{:S(2)}) collective-permute-start(bf16[8,3072]{1,0:T(8,128)(2,1)S(1)} %get-tuple-element.15), channel_id=1, source_target_pairs={{0,4},{4,8},{8,12},{12,16},{16,20},{20,24},{24,28},{28,0},{1,5},{5... | collective-permute-start | bytes 147464 | tf_op jit(solution)/shard_map/ppermute | solution.py:20
  125.7 4.6 %collective-permute-start.12 = (bf16[8,3072]{1,0:T(8,128)(2,1)S(1)}, bf16[8,3072]{1,0:T(8,128)(2,1)S(1)}, u32[]{:S(2)}, u32[]{:S(2)}) collective-permute-start(bf16[8,3072]{1,0:T(8,128)(2,1)S(1)} %get-tuple-element.16), channel_id=1, source_target_pairs={{0,0},{4,4},{8,8},{12,12},{16,16},{20,20},{24,24},{28,28},{1,1},{5... | collective-permute-start | bytes 147464 | tf_op jit(solution)/shard_map/ppermute | solution.py:20
  125.7 4.6 %collective-permute-start.11 = (bf16[8,3072]{1,0:T(8,128)(2,1)S(1)}, bf16[8,3072]{1,0:T(8,128)(2,1)S(1)}, u32[]{:S(2)}, u32[]{:S(2)}) collective-permute-start(bf16[8,3072]{1,0:T(8,128)(2,1)S(1)} %get-tuple-element.17), channel_id=1, source_target_pairs={{0,28},{4,0},{8,4},{12,8},{16,12},{20,16},{24,20},{28,24},{1,29},{... | collective-permute-start | bytes 147464 | tf_op jit(solution)/shard_map/ppermute | solution.py:20
  132.5 6.5 %collective-permute-start.15 = (bf16[8,3072]{1,0:T(8,128)(2,1)S(1)}, bf16[8,3072]{1,0:T(8,128)(2,1)S(1)}, u32[]{:S(2)}, u32[]{:S(2)}) collective-permute-start(bf16[8,3072]{1,0:T(8,128)(2,1)S(1)} %get-tuple-element.13), channel_id=1, source_target_pairs={{0,8},{4,12},{8,16},{12,20},{16,24},{20,28},{24,0},{28,4},{1,9},{5... | collective-permute-start | bytes 147464 | tf_op jit(solution)/shard_map/ppermute | solution.py:20
  133.4 10.6 %collective-permute-start.19 = (bf16[8,3072]{1,0:T(8,128)(2,1)S(1)}, bf16[8,3072]{1,0:T(8,128)(2,1)S(1)}, u32[]{:S(2)}, u32[]{:S(2)}) collective-permute-start(bf16[8,3072]{1,0:T(8,128)(2,1)S(1)} %get-tuple-element.9), channel_id=1, source_target_pairs={{0,24},{4,28},{8,0},{12,4},{16,8},{20,12},{24,16},{28,20},{1,25},{... | collective-permute-start | bytes 147464 | tf_op jit(solution)/shard_map/ppermute | solution.py:20
  134.6 9.4 %collective-permute-start.18 = (bf16[8,3072]{1,0:T(8,128)(2,1)S(1)}, bf16[8,3072]{1,0:T(8,128)(2,1)S(1)}, u32[]{:S(2)}, u32[]{:S(2)}) collective-permute-start(bf16[8,3072]{1,0:T(8,128)(2,1)S(1)} %get-tuple-element.10), channel_id=1, source_target_pairs={{0,28},{4,0},{8,4},{12,8},{16,12},{20,16},{24,20},{28,24},{1,29},{... | collective-permute-start | bytes 147464 | tf_op jit(solution)/shard_map/ppermute | solution.py:20
  138.9 5.0 %collective-permute-start.17 = (bf16[8,3072]{1,0:T(8,128)(2,1)S(1)}, bf16[8,3072]{1,0:T(8,128)(2,1)S(1)}, u32[]{:S(2)}, u32[]{:S(2)}) collective-permute-start(bf16[8,3072]{1,0:T(8,128)(2,1)S(1)} %get-tuple-element.11), channel_id=1, source_target_pairs={{0,0},{4,4},{8,8},{12,12},{16,16},{20,20},{24,24},{28,28},{1,1},{5... | collective-permute-start | bytes 147464 | tf_op jit(solution)/shard_map/ppermute | solution.py:20
  138.9 5.0 %collective-permute-start.16 = (bf16[8,3072]{1,0:T(8,128)(2,1)S(1)}, bf16[8,3072]{1,0:T(8,128)(2,1)S(1)}, u32[]{:S(2)}, u32[]{:S(2)}) collective-permute-start(bf16[8,3072]{1,0:T(8,128)(2,1)S(1)} %get-tuple-element.12), channel_id=1, source_target_pairs={{0,4},{4,8},{8,12},{12,16},{16,20},{20,24},{24,28},{28,0},{1,5},{5... | collective-permute-start | bytes 147464 | tf_op jit(solution)/shard_map/ppermute | solution.py:20
  153.0 44.9 %copy-start.2 = (f32[512,192]{0,1:T(8,128)S(1)}, f32[512,192]{0,1:T(8,128)}, u32[]{:S(2)}) copy-start(f32[512,192]{0,1:T(8,128)} %get-tuple-element.34) | copy-start | bytes 1179652
  (6 other events, 35.0 us)
where the time goes:
time: 200 us; the launch traced here: 199 us
  blocking collectives  118 us (59%)
  starting transfers between devices  32.3 us (16%)
  waiting for transfers between devices  18.9 us (9%)
  local copies, waits for them, and re-layouts  17.4 us (9%)
  matrix products  9.63 us (5%)
  other arithmetic  2.44 us (1%)
    psum x2, blocking collectives, body(): vertex = lax.psum(spread, ('sub', 'grp'))  86.7 us
    ppermute x20, starting transfers between devices, passed_along(): return lax.ppermute(value, axis, pairs)  23.8 us
    ppermute x20, waiting for transfers between devices, passed_along(): return lax.ppermute(value, axis, pairs)  15.9 us
    all_gather x2, blocking collectives, body(): lax.all_gather(trace_b, 'grp', axis=0, tiled=True)  15.4 us
    all_to_all x1, blocking collectives, body(): lax.all_to_all(coeffs, 'grp', split_axis=2, concat_axis=0, tiled=True)  7.97 us
    all_to_all x1, blocking collectives, body(): lax.all_to_all(own_back.reshape(all_faces, MODES, part_rhs), 'grp', split...  7.64 us
    all_to_all x1, starting transfers between devices, body(): lax.all_to_all(coeffs, 'grp', split_axis=2, concat_axis=0, tiled=True)  4.28 us
    all_to_all x1, starting transfers between devices, body(): lax.all_to_all(own_back.reshape(all_faces, MODES, part_rhs), 'grp', split...  4.26 us
  transfers between devices with their start and end apart: 22, of which 6 were waited for; matrix products, arithmetic and copies ran while one was open for 3% of the time, Pallas kernels for 0%

commit v1 on v0

--- a/solution.py
+++ b/solution.py
@@ -137,7 +137,9 @@
         ).reshape(own_rows, -1)
         partial_value = jnp.dot(coarse_wide, lifted, precision=highest)
         spread = lax.dot_general(corner_hot, partial_value, contract_first, precision=highest)
-        vertex = lax.psum(spread, ("sub", "grp"))
+        vertex = spread
+        for at in ("grp", "sub"):
+            vertex = jax.lax.psum(vertex, axis_name=at)
         picked = jnp.dot(corner_hot, vertex, precision=highest)
         coarse_corr = lax.dot_general(coarse_wide, picked, contract_first, precision=highest)
         traces = traces - relax_weight * lifted - coarse_weight * coarse_corr

time: 200 us -> 209 us (1.045)
  the two profiles are of different devices: /device:TPU:10 before, /device:TPU:0 now
where the time goes in v1:
time: 209 us
  blocking collectives  119 us (57%)
  starting transfers between devices  35.4 us (17%)
  waiting for transfers between devices  23.4 us (11%)
  local copies, waits for them, and re-layouts  17.4 us (8%)
  matrix products  9.64 us (5%)
  other arithmetic  2.46 us (1%)
    psum x4, blocking collectives, body(): vertex = jax.lax.psum(vertex, axis_name=at)  86.2 us
    ppermute x20, starting transfers between devices, passed_along(): return lax.ppermute(value, axis, pairs)  28.7 us
    ppermute x20, waiting for transfers between devices, passed_along(): return lax.ppermute(value, axis, pairs)  18.1 us
    all_gather x2, blocking collectives, body(): lax.all_gather(trace_b, 'grp', axis=0, tiled=True)  17.9 us
    all_to_all x1, blocking collectives, body(): lax.all_to_all(coeffs, 'grp', split_axis=2, concat_axis=0, tiled=True)  7.67 us
    all_to_all x1, blocking collectives, body(): lax.all_to_all(own_back.reshape(all_faces, MODES, part_rhs), 'grp', split...  7.67 us
    all_to_all x1, waiting for transfers between devices, body(): lax.all_to_all(own_back.reshape(all_faces, MODES, part_rhs), 'grp', split...  4.46 us
  transfers between devices with their start and end apart: 22, of which 8 were waited for; matrix products, arithmetic and copies ran while one was open for 3% of the time, Pallas kernels for 0%

profile of v1, /device:TPU:0, one launch (start us, length us, event | category | flops | bytes accessed | tf_op | source)
XLA Modules:
  0.0 208.6 jit_solution(8793378378266768691)
XLA Ops:
  0.0 1.2 reshape_squeeze.3
  1.2 1.0 bitcast_convert_fusion
  2.2 10.1 %all_gather.6 = bf16[2048,192]{0,1:T(8,128)(2,1)S(1)} all-gather(bf16[512,192]{0,1:T(8,128)(2,1)S(1)} %bitcast_convert_fusion), channel_id=1, replica_groups=mesh['sub'=8,'grp'=4] {'grp'}, dimensions={0}, use_global_device_ids=true | all-gather | bytes 983040 | tf_op jit(solution)/shard_map/all_gather | solution.py:94
  12.3 1.8 fusion.20
  14.8 1.0 reshape.310
  15.8 3.4 %all-to-all-start = ((bf16[4,2,12288]{2,1,0:T(2,128)(2,1)}), bf16[4,2,12288]{2,1,0:T(2,128)(2,1)S(1)}, u32[]{:S(2)}, u32[]{:S(2)}) async-start(bf16[4,2,12288]{2,1,0:T(2,128)(2,1)} %reshape.310), calls=%async_computation | async-start | bytes 393216 | tf_op jit(solution)/shard_map/all_to_all | solution.py:102
  23.5 0.9 all-to-all-done
  26.1 3.6 %collective-permute-start = (bf16[8,3072]{1,0:T(8,128)(2,1)S(1)}, bf16[8,3072]{1,0:T(8,128)(2,1)S(1)}, u32[]{:S(2)}, u32[]{:S(2)}) collective-permute-start(bf16[8,3072]{1,0:T(8,128)(2,1)S(1)} %get-tuple-element.28), channel_id=1, source_target_pairs={{0,24},{4,28},{8,0},{12,4},{16,8},{20,12},{24,16},{28,20},{1,25},{... | collective-permute-start | bytes 147464 | tf_op jit(solution)/shard_map/ppermute | solution.py:20
  29.9 1.6 collective-permute-start.3
  31.4 3.3 %collective-permute-start.1 = (bf16[8,3072]{1,0:T(8,128)(2,1)S(1)}, bf16[8,3072]{1,0:T(8,128)(2,1)S(1)}, u32[]{:S(2)}, u32[]{:S(2)}) collective-permute-start(bf16[8,3072]{1,0:T(8,128)(2,1)S(1)} %get-tuple-element.27), channel_id=1, source_target_pairs={{0,28},{4,0},{8,4},{12,8},{16,12},{20,16},{24,20},{28,24},{1,29},{... | collective-permute-start | bytes 147464 | tf_op jit(solution)/shard_map/ppermute | solution.py:20
  34.7 1.7 collective-permute-done.1
  40.0 3.9 %collective-permute-start.9 = (bf16[8,3072]{1,0:T(8,128)(2,1)S(1)}, bf16[8,3072]{1,0:T(8,128)(2,1)S(1)}, u32[]{:S(2)}, u32[]{:S(2)}) collective-permute-start(bf16[8,3072]{1,0:T(8,128)(2,1)S(1)} %get-tuple-element.19), channel_id=1, source_target_pairs={{0,24},{4,28},{8,0},{12,4},{16,8},{20,12},{24,16},{28,20},{1,25},{... | collective-permute-start | bytes 147464 | tf_op jit(solution)/shard_map/ppermute | solution.py:20
  43.9 2.5 %collective-permute-start.8 = (bf16[8,3072]{1,0:T(8,128)(2,1)S(1)}, bf16[8,3072]{1,0:T(8,128)(2,1)S(1)}, u32[]{:S(2)}, u32[]{:S(2)}) collective-permute-start(bf16[8,3072]{1,0:T(8,128)(2,1)S(1)} %get-tuple-element.20), channel_id=1, source_target_pairs={{0,28},{4,0},{8,4},{12,8},{16,12},{20,16},{24,20},{28,24},{1,29},{... | collective-permute-start | bytes 147464 | tf_op jit(solution)/shard_map/ppermute | solution.py:20
  46.4 6.8 %collective-permute-done.6 = bf16[8,3072]{1,0:T(8,128)(2,1)S(1)} collective-permute-done((bf16[8,3072]{1,0:T(8,128)(2,1)S(1)}, bf16[8,3072]{1,0:T(8,128)(2,1)S(1)}, u32[]{:S(2)}, u32[]{:S(2)}) %collective-permute-start.6) | collective-permute-done | bytes 49184 | tf_op jit(solution)/shard_map/ppermute | solution.py:20
  54.3 1.0 reshape.312
  55.3 3.4 %all-to-all-start.1 = ((bf16[4,2,12288]{2,1,0:T(2,128)(2,1)}), bf16[4,2,12288]{2,1,0:T(2,128)(2,1)S(1)}, u32[]{:S(2)}, u32[]{:S(2)}) async-start(bf16[4,2,12288]{2,1,0:T(2,128)(2,1)} %reshape.312), calls=%async_computation.1 | async-start | bytes 393216 | tf_op jit(solution)/shard_map/all_to_all | solution.py:128
  59.5 4.5 %all-to-all-done.1 = bf16[4,2,12288]{2,1,0:T(2,128)(2,1)S(1)} async-done(((bf16[4,2,12288]{2,1,0:T(2,128)(2,1)}), bf16[4,2,12288]{2,1,0:T(2,128)(2,1)S(1)}, u32[]{:S(2)}, u32[]{:S(2)}) %all-to-all-start.1) | async-done | bytes 196640 | tf_op jit(solution)/shard_map/all_to_all | solution.py:128
  65.4 10.1 %psum.28 = f32[16,192]{1,0:T(8,128)S(1)} all-reduce(f32[16,192]{1,0:T(8,128)S(1)} %fusion.55), channel_id=1, replica_groups=mesh['sub'=8,'grp'=4] {'grp'}, use_global_device_ids=true, to_apply=%region_1.0 | all-reduce | flops 3072 | bytes 24576 | tf_op jit(solution)/shard_map/psum | solution.py:142
  75.5 33.0 %psum.29 = f32[16,192]{1,0:T(8,128)S(1)} all-reduce(f32[16,192]{1,0:T(8,128)S(1)} %psum.28), channel_id=1, replica_groups=mesh['sub'=8,'grp'=4] {'sub'}, use_global_device_ids=true, to_apply=%region_2.5 | all-reduce | flops 3072 | bytes 24576 | tf_op jit(solution)/shard_map/psum | solution.py:142
  108.7 1.1 fusion.72
  109.8 7.9 %all_gather.7 = bf16[2048,192]{0,1:T(8,128)(2,1)S(1)} all-gather(bf16[512,192]{0,1:T(8,128)(2,1)S(1)} %get-tuple-element.33), channel_id=1, replica_groups=mesh['sub'=8,'grp'=4] {'grp'}, dimensions={0}, use_global_device_ids=true | all-gather | bytes 983040 | tf_op jit(solution)/shard_map/all_gather | solution.py:94
  119.5 7.7 %all_to_all.66 = bf16[4,2,12288]{2,1,0:T(2,128)(2,1)S(1)} all-to-all(bf16[4,2,12288]{2,1,0:T(2,128)(2,1)S(1)} %reshape.314), channel_id=1, replica_groups=mesh['sub'=8,'grp'=4] {'grp'}, dimensions={0} | all-to-all | bytes 393216 | tf_op jit(solution)/shard_map/all_to_all | solution.py:102
  128.9 2.0 collective-permute-start.14
  130.9 4.7 %collective-permute-start.11 = (bf16[8,3072]{1,0:T(8,128)(2,1)S(1)}, bf16[8,3072]{1,0:T(8,128)(2,1)S(1)}, u32[]{:S(2)}, u32[]{:S(2)}) collective-permute-start(bf16[8,3072]{1,0:T(8,128)(2,1)S(1)} %get-tuple-element.17), channel_id=1, source_target_pairs={{0,28},{4,0},{8,4},{12,8},{16,12},{20,16},{24,20},{28,24},{1,29},{... | collective-permute-start | bytes 147464 | tf_op jit(solution)/shard_map/ppermute | solution.py:20
  135.7 1.7 collective-permute-done.11
  139.9 3.8 %collective-permute-start.19 = (bf16[8,3072]{1,0:T(8,128)(2,1)S(1)}, bf16[8,3072]{1,0:T(8,128)(2,1)S(1)}, u32[]{:S(2)}, u32[]{:S(2)}) collective-permute-start(bf16[8,3072]{1,0:T(8,128)(2,1)S(1)} %get-tuple-element.9), channel_id=1, source_target_pairs={{0,24},{4,28},{8,0},{12,4},{16,8},{20,12},{24,16},{28,20},{1,25},{... | collective-permute-start | bytes 147464 | tf_op jit(solution)/shard_map/ppermute | solution.py:20
  143.7 3.1 %collective-permute-start.18 = (bf16[8,3072]{1,0:T(8,128)(2,1)S(1)}, bf16[8,3072]{1,0:T(8,128)(2,1)S(1)}, u32[]{:S(2)}, u32[]{:S(2)}) collective-permute-start(bf16[8,3072]{1,0:T(8,128)(2,1)S(1)} %get-tuple-element.10), channel_id=1, source_target_pairs={{0,28},{4,0},{8,4},{12,8},{16,12},{20,16},{24,20},{28,24},{1,29},{... | collective-permute-start | bytes 147464 | tf_op jit(solution)/shard_map/ppermute | solution.py:20
  146.9 6.8 %collective-permute-done.16 = bf16[8,3072]{1,0:T(8,128)(2,1)S(1)} collective-permute-done((bf16[8,3072]{1,0:T(8,128)(2,1)S(1)}, bf16[8,3072]{1,0:T(8,128)(2,1)S(1)}, u32[]{:S(2)}, u32[]{:S(2)}) %collective-permute-start.16) | collective-permute-done | bytes 49184 | tf_op jit(solution)/shard_map/ppermute | solution.py:20
  155.1 7.7 %all_to_all.67 = bf16[4,2,12288]{2,1,0:T(2,128)(2,1)S(1)} all-to-all(bf16[4,2,12288]{2,1,0:T(2,128)(2,1)S(1)} %reshape.316), channel_id=1, replica_groups=mesh['sub'=8,'grp'=4] {'grp'}, dimensions={0} | all-to-all | bytes 393216 | tf_op jit(solution)/shard_map/all_to_all | solution.py:128
  164.2 10.1 %psum.30 = f32[16,192]{1,0:T(8,128)S(1)} all-reduce(f32[16,192]{1,0:T(8,128)S(1)} %fusion.53), channel_id=1, replica_groups=mesh['sub'=8,'grp'=4] {'grp'}, use_global_device_ids=true, to_apply=%region_3.6 | all-reduce | flops 3072 | bytes 24576 | tf_op jit(solution)/shard_map/psum | solution.py:142
  174.3 33.0 %psum.31 = f32[16,192]{1,0:T(8,128)S(1)} all-reduce(f32[16,192]{1,0:T(8,128)S(1)} %psum.30), channel_id=1, replica_groups=mesh['sub'=8,'grp'=4] {'sub'}, use_global_device_ids=true, to_apply=%region_4.7 | all-reduce | flops 3072 | bytes 24576 | tf_op jit(solution)/shard_map/psum | solution.py:142
  207.5 1.1 fusion.6
  (156 shorter events, 22.5 us)
Async XLA Ops:
  0.0 12.3 %copy-start = (bf16[1,512,2048]{2,1,0:T(8,128)(2,1)S(1)}, bf16[1,512,2048]{2,1,0:T(8,128)(2,1)}, u32[]{:S(2)}) copy-start(bf16[1,512,2048]{2,1,0:T(8,128)(2,1)} %param.14) | copy-start | bytes 6291460
  15.8 8.6 %all-to-all-start = ((bf16[4,2,12288]{2,1,0:T(2,128)(2,1)}), bf16[4,2,12288]{2,1,0:T(2,128)(2,1)S(1)}, u32[]{:S(2)}, u32[]{:S(2)}) async-start(bf16[4,2,12288]{2,1,0:T(2,128)(2,1)} %reshape.310), calls=%async_computation | async-start | bytes 393216 | tf_op jit(solution)/shard_map/all_to_all | solution.py:102
  23.4 15.7 %copy-start.8 = (bf16[5,8,16]{2,1,0:T(8,128)(2,1)}, bf16[5,8,16]{2,1,0:T(8,128)(2,1)S(1)}, u32[]{:S(2)}) copy-start(bf16[5,8,16]{2,1,0:T(8,128)(2,1)S(1)} %convolution_convert_fusion.8) | copy-start | bytes 3844
  23.5 14.8 %copy-start.10 = (f32[16,64]{1,0:T(8,128)}, f32[16,64]{1,0:T(8,128)S(1)}, u32[]{:S(2)}) copy-start(f32[16,64]{1,0:T(8,128)S(1)} %and_convert_fusion) | copy-start | bytes 12292
  26.1 8.6 %collective-permute-start = (bf16[8,3072]{1,0:T(8,128)(2,1)S(1)}, bf16[8,3072]{1,0:T(8,128)(2,1)S(1)}, u32[]{:S(2)}, u32[]{:S(2)}) collective-permute-start(bf16[8,3072]{1,0:T(8,128)(2,1)S(1)} %get-tuple-element.28), channel_id=1, source_target_pairs={{0,24},{4,28},{8,0},{12,4},{16,8},{20,12},{24,16},{28,20},{1,25},{... | collective-permute-start | bytes 147464 | tf_op jit(solution)/shard_map/ppermute | solution.py:20
  29.9 7.4 %collective-permute-start.4 = (bf16[8,3072]{1,0:T(8,128)(2,1)S(1)}, bf16[8,3072]{1,0:T(8,128)(2,1)S(1)}, u32[]{:S(2)}, u32[]{:S(2)}) collective-permute-start(bf16[8,3072]{1,0:T(8,128)(2,1)S(1)} %get-tuple-element.24), channel_id=1, source_target_pairs={{0,8},{4,12},{8,16},{12,20},{16,24},{20,28},{24,0},{28,4},{1,9},{5... | collective-permute-start | bytes 147464 | tf_op jit(solution)/shard_map/ppermute | solution.py:20
  29.9 7.4 %collective-permute-start.3 = (bf16[8,3072]{1,0:T(8,128)(2,1)S(1)}, bf16[8,3072]{1,0:T(8,128)(2,1)S(1)}, u32[]{:S(2)}, u32[]{:S(2)}) collective-permute-start(bf16[8,3072]{1,0:T(8,128)(2,1)S(1)} %get-tuple-element.25), channel_id=1, source_target_pairs={{0,4},{4,8},{8,12},{12,16},{16,20},{20,24},{24,28},{28,0},{1,5},{5... | collective-permute-start | bytes 147464 | tf_op jit(solution)/shard_map/ppermute | solution.py:20
  31.4 5.1 %collective-permute-start.2 = (bf16[8,3072]{1,0:T(8,128)(2,1)S(1)}, bf16[8,3072]{1,0:T(8,128)(2,1)S(1)}, u32[]{:S(2)}, u32[]{:S(2)}) collective-permute-start(bf16[8,3072]{1,0:T(8,128)(2,1)S(1)} %get-tuple-element.26), channel_id=1, source_target_pairs={{0,0},{4,4},{8,8},{12,12},{16,16},{20,20},{24,24},{28,28},{1,1},{5... | collective-permute-start | bytes 147464 | tf_op jit(solution)/shard_map/ppermute | solution.py:20
  31.4 5.0 %collective-permute-start.1 = (bf16[8,3072]{1,0:T(8,128)(2,1)S(1)}, bf16[8,3072]{1,0:T(8,128)(2,1)S(1)}, u32[]{:S(2)}, u32[]{:S(2)}) collective-permute-start(bf16[8,3072]{1,0:T(8,128)(2,1)S(1)} %get-tuple-element.27), channel_id=1, source_target_pairs={{0,28},{4,0},{8,4},{12,8},{16,12},{20,16},{24,20},{28,24},{1,29},{... | collective-permute-start | bytes 147464 | tf_op jit(solution)/shard_map/ppermute | solution.py:20
  39.4 7.0 %collective-permute-start.5 = (bf16[8,3072]{1,0:T(8,128)(2,1)S(1)}, bf16[8,3072]{1,0:T(8,128)(2,1)S(1)}, u32[]{:S(2)}, u32[]{:S(2)}) collective-permute-start(bf16[8,3072]{1,0:T(8,128)(2,1)S(1)} %get-tuple-element.23), channel_id=1, source_target_pairs={{0,8},{4,12},{8,16},{12,20},{16,24},{20,28},{24,0},{28,4},{1,9},{5... | collective-permute-start | bytes 147464 | tf_op jit(solution)/shard_map/ppermute | solution.py:20
  40.0 13.2 %collective-permute-start.9 = (bf16[8,3072]{1,0:T(8,128)(2,1)S(1)}, bf16[8,3072]{1,0:T(8,128)(2,1)S(1)}, u32[]{:S(2)}, u32[]{:S(2)}) collective-permute-start(bf16[8,3072]{1,0:T(8,128)(2,1)S(1)} %get-tuple-element.19), channel_id=1, source_target_pairs={{0,24},{4,28},{8,0},{12,4},{16,8},{20,12},{24,16},{28,20},{1,25},{... | collective-permute-start | bytes 147464 | tf_op jit(solution)/shard_map/ppermute | solution.py:20
  43.9 9.3 %collective-permute-start.8 = (bf16[8,3072]{1,0:T(8,128)(2,1)S(1)}, bf16[8,3072]{1,0:T(8,128)(2,1)S(1)}, u32[]{:S(2)}, u32[]{:S(2)}) collective-permute-start(bf16[8,3072]{1,0:T(8,128)(2,1)S(1)} %get-tuple-element.20), channel_id=1, source_target_pairs={{0,28},{4,0},{8,4},{12,8},{16,12},{20,16},{24,20},{28,24},{1,29},{... | collective-permute-start | bytes 147464 | tf_op jit(solution)/shard_map/ppermute | solution.py:20
  46.4 6.8 %collective-permute-start.7 = (bf16[8,3072]{1,0:T(8,128)(2,1)S(1)}, bf16[8,3072]{1,0:T(8,128)(2,1)S(1)}, u32[]{:S(2)}, u32[]{:S(2)}) collective-permute-start(bf16[8,3072]{1,0:T(8,128)(2,1)S(1)} %get-tuple-element.21), channel_id=1, source_target_pairs={{0,0},{4,4},{8,8},{12,12},{16,16},{20,20},{24,24},{28,28},{1,1},{5... | collective-permute-start | bytes 147464 | tf_op jit(solution)/shard_map/ppermute | solution.py:20
  46.4 6.8 %collective-permute-start.6 = (bf16[8,3072]{1,0:T(8,128)(2,1)S(1)}, bf16[8,3072]{1,0:T(8,128)(2,1)S(1)}, u32[]{:S(2)}, u32[]{:S(2)}) collective-permute-start(bf16[8,3072]{1,0:T(8,128)(2,1)S(1)} %get-tuple-element.22), channel_id=1, source_target_pairs={{0,4},{4,8},{8,12},{12,16},{16,20},{20,24},{24,28},{28,0},{1,5},{5... | collective-permute-start | bytes 147464 | tf_op jit(solution)/shard_map/ppermute | solution.py:20
  54.3 10.6 %copy-start.7 = (bf16[1,8,512]{2,1,0:T(8,128)(2,1)S(1)}, bf16[1,8,512]{2,1,0:T(8,128)(2,1)}, u32[]{:S(2)}) copy-start(bf16[1,8,512]{2,1,0:T(8,128)(2,1)} %param.18) | copy-start | bytes 24580
  55.3 8.6 %all-to-all-start.1 = ((bf16[4,2,12288]{2,1,0:T(2,128)(2,1)}), bf16[4,2,12288]{2,1,0:T(2,128)(2,1)S(1)}, u32[]{:S(2)}, u32[]{:S(2)}) async-start(bf16[4,2,12288]{2,1,0:T(2,128)(2,1)} %reshape.312), calls=%async_computation.1 | async-start | bytes 393216 | tf_op jit(solution)/shard_map/all_to_all | solution.py:128
  58.7 50.0 %copy-start.1 = (f32[1,512,192]{1,2,0:T(8,128)S(1)}, f32[1,512,192]{1,2,0:T(8,128)}, u32[]{:S(2)}) copy-start(f32[1,512,192]{1,2,0:T(8,128)} %param.16) | copy-start | bytes 1179652
  108.5 9.2 %copy-start.3 = (f32[1,512,192]{1,2,0:T(8,128)S(1)}, f32[1,512,192]{1,2,0:T(8,128)}, u32[]{:S(2)}) copy-start(f32[1,512,192]{1,2,0:T(8,128)} %param.15) | copy-start | bytes 1179652
  127.8 11.0 %copy-start.9 = (bf16[5,8,16]{2,1,0:T(8,128)(2,1)S(1)}, bf16[5,8,16]{2,1,0:T(8,128)(2,1)}, u32[]{:S(2)}) copy-start(bf16[5,8,16]{2,1,0:T(8,128)(2,1)} %copy-done.8) | copy-start | bytes 3844
  127.8 11.0 %copy-start.11 = (f32[16,64]{1,0:T(8,128)S(1)}, f32[16,64]{1,0:T(8,128)}, u32[]{:S(2)}) copy-start(f32[16,64]{1,0:T(8,128)} %copy-done.10) | copy-start | bytes 12292
  127.8 11.0 %copy-start.15 = (f32[16]{0:T(128)S(1)}, f32[16]{0:T(128)}, u32[]{:S(2)}) copy-start(f32[16]{0:T(128)} %copy-done.14) | copy-start | bytes 196
  128.8 6.8 %collective-permute-start.10 = (bf16[8,3072]{1,0:T(8,128)(2,1)S(1)}, bf16[8,3072]{1,0:T(8,128)(2,1)S(1)}, u32[]{:S(2)}, u32[]{:S(2)}) collective-permute-start(bf16[8,3072]{1,0:T(8,128)(2,1)S(1)} %get-tuple-element.18), channel_id=1, source_target_pairs={{0,24},{4,28},{8,0},{12,4},{16,8},{20,12},{24,16},{28,20},{1,25},{... | collective-permute-start | bytes 147464 | tf_op jit(solution)/shard_map/ppermute | solution.py:20
  128.9 8.8 %collective-permute-start.14 = (bf16[8,3072]{1,0:T(8,128)(2,1)S(1)}, bf16[8,3072]{1,0:T(8,128)(2,1)S(1)}, u32[]{:S(2)}, u32[]{:S(2)}) collective-permute-start(bf16[8,3072]{1,0:T(8,128)(2,1)S(1)} %get-tuple-element.14), channel_id=1, source_target_pairs={{0,8},{4,12},{8,16},{12,20},{16,24},{20,28},{24,0},{28,4},{1,9},{5... | collective-permute-start | bytes 147464 | tf_op jit(solution)/shard_map/ppermute | solution.py:20
  130.9 6.8 %collective-permute-start.13 = (bf16[8,3072]{1,0:T(8,128)(2,1)S(1)}, bf16[8,3072]{1,0:T(8,128)(2,1)S(1)}, u32[]{:S(2)}, u32[]{:S(2)}) collective-permute-start(bf16[8,3072]{1,0:T(8,128)(2,1)S(1)} %get-tuple-element.15), channel_id=1, source_target_pairs={{0,4},{4,8},{8,12},{12,16},{16,20},{20,24},{24,28},{28,0},{1,5},{5... | collective-permute-start | bytes 147464 | tf_op jit(solution)/shard_map/ppermute | solution.py:20
  130.9 6.5 %collective-permute-start.12 = (bf16[8,3072]{1,0:T(8,128)(2,1)S(1)}, bf16[8,3072]{1,0:T(8,128)(2,1)S(1)}, u32[]{:S(2)}, u32[]{:S(2)}) collective-permute-start(bf16[8,3072]{1,0:T(8,128)(2,1)S(1)} %get-tuple-element.16), channel_id=1, source_target_pairs={{0,0},{4,4},{8,8},{12,12},{16,16},{20,20},{24,24},{28,28},{1,1},{5... | collective-permute-start | bytes 147464 | tf_op jit(solution)/shard_map/ppermute | solution.py:20
  130.9 6.5 %collective-permute-start.11 = (bf16[8,3072]{1,0:T(8,128)(2,1)S(1)}, bf16[8,3072]{1,0:T(8,128)(2,1)S(1)}, u32[]{:S(2)}, u32[]{:S(2)}) collective-permute-start(bf16[8,3072]{1,0:T(8,128)(2,1)S(1)} %get-tuple-element.17), channel_id=1, source_target_pairs={{0,28},{4,0},{8,4},{12,8},{16,12},{20,16},{24,20},{28,24},{1,29},{... | collective-permute-start | bytes 147464 | tf_op jit(solution)/shard_map/ppermute | solution.py:20
  139.9 7.0 %collective-permute-start.15 = (bf16[8,3072]{1,0:T(8,128)(2,1)S(1)}, bf16[8,3072]{1,0:T(8,128)(2,1)S(1)}, u32[]{:S(2)}, u32[]{:S(2)}) collective-permute-start(bf16[8,3072]{1,0:T(8,128)(2,1)S(1)} %get-tuple-element.13), channel_id=1, source_target_pairs={{0,8},{4,12},{8,16},{12,20},{16,24},{20,28},{24,0},{28,4},{1,9},{5... | collective-permute-start | bytes 147464 | tf_op jit(solution)/shard_map/ppermute | solution.py:20
  139.9 13.7 %collective-permute-start.19 = (bf16[8,3072]{1,0:T(8,128)(2,1)S(1)}, bf16[8,3072]{1,0:T(8,128)(2,1)S(1)}, u32[]{:S(2)}, u32[]{:S(2)}) collective-permute-start(bf16[8,3072]{1,0:T(8,128)(2,1)S(1)} %get-tuple-element.9), channel_id=1, source_target_pairs={{0,24},{4,28},{8,0},{12,4},{16,8},{20,12},{24,16},{28,20},{1,25},{... | collective-permute-start | bytes 147464 | tf_op jit(solution)/shard_map/ppermute | solution.py:20
  143.7 9.9 %collective-permute-start.18 = (bf16[8,3072]{1,0:T(8,128)(2,1)S(1)}, bf16[8,3072]{1,0:T(8,128)(2,1)S(1)}, u32[]{:S(2)}, u32[]{:S(2)}) collective-permute-start(bf16[8,3072]{1,0:T(8,128)(2,1)S(1)} %get-tuple-element.10), channel_id=1, source_target_pairs={{0,28},{4,0},{8,4},{12,8},{16,12},{20,16},{24,20},{28,24},{1,29},{... | collective-permute-start | bytes 147464 | tf_op jit(solution)/shard_map/ppermute | solution.py:20
  146.8 6.8 %collective-permute-start.17 = (bf16[8,3072]{1,0:T(8,128)(2,1)S(1)}, bf16[8,3072]{1,0:T(8,128)(2,1)S(1)}, u32[]{:S(2)}, u32[]{:S(2)}) collective-permute-start(bf16[8,3072]{1,0:T(8,128)(2,1)S(1)} %get-tuple-element.11), channel_id=1, source_target_pairs={{0,0},{4,4},{8,8},{12,12},{16,16},{20,20},{24,24},{28,28},{1,1},{5... | collective-permute-start | bytes 147464 | tf_op jit(solution)/shard_map/ppermute | solution.py:20
  146.8 6.8 %collective-permute-start.16 = (bf16[8,3072]{1,0:T(8,128)(2,1)S(1)}, bf16[8,3072]{1,0:T(8,128)(2,1)S(1)}, u32[]{:S(2)}, u32[]{:S(2)}) collective-permute-start(bf16[8,3072]{1,0:T(8,128)(2,1)S(1)} %get-tuple-element.12), channel_id=1, source_target_pairs={{0,4},{4,8},{8,12},{12,16},{16,20},{20,24},{24,28},{28,0},{1,5},{5... | collective-permute-start | bytes 147464 | tf_op jit(solution)/shard_map/ppermute | solution.py:20
  162.7 44.7 %copy-start.2 = (f32[512,192]{0,1:T(8,128)S(1)}, f32[512,192]{0,1:T(8,128)}, u32[]{:S(2)}) copy-start(f32[512,192]{0,1:T(8,128)} %get-tuple-element.34) | copy-start | bytes 1179652
  (6 other events, 31.8 us)
